TPU v7x, 32 devices: a whole 2x2x4 slice. The times are simulated.
32 devices in a mesh: pipe: 4 (over z), dp: 4 (over x, core), expert: 2 (over y).
Axes of the slice: x: 2, y: 2, z: 4, core: 2. Of those that a mesh axis runs over, the one named last changes fastest.
Arguments:
- block_input: bfloat16 [4, 1024, 3072], P('pipe', ('dp', 'expert')), may hold values from -6 to 6
- output_grad: bfloat16 [4, 1024, 3072], P('pipe', ('dp', 'expert')), may hold values from -6 to 6
- expert_ids: int32 [4, 1024, 6], P('pipe', ('dp', 'expert')), may hold values from 0 to 159, all different within a row
- gate_weights: float32 [4, 1024, 6], P('pipe', ('dp', 'expert')), may hold values from 0.25 to 2
- gate_proj: bfloat16 [4, 2, 3072, 1024], P('pipe', 'expert', None, 'dp'), may hold values from -0.109375 to 0.109375
- up_proj: bfloat16 [4, 2, 3072, 1024], P('pipe', 'expert', None, 'dp'), may hold values from -0.109375 to 0.109375
- down_proj: bfloat16 [4, 2, 1024, 3072], P('pipe', 'expert', 'dp'), may hold values from -0.1875 to 0.1875
Outputs:
- received_grad: bfloat16 [4, 1024, 3072], P('pipe', ('dp', 'expert'))
- gate_weight_grad: float32 [4, 1024, 6], P('pipe', ('dp', 'expert'))
- gate_proj_grad: bfloat16 [4, 2, 3072, 1024], P('pipe', 'expert', None, 'dp')
- up_proj_grad: bfloat16 [4, 2, 3072, 1024], P('pipe', 'expert', None, 'dp')
- down_proj_grad: bfloat16 [4, 2, 1024, 3072], P('pipe', 'expert', 'dp')
Inputs may be any that keep to these rules, and one draw needn't show every extreme that they name: `expert_ids`: each token names 6 different experts.
All inputs are finite; a program needn't handle non-finite values.
Results may differ from a plain program's by a relative error of at most 0.006.
Values may be sent and summed in bfloat16 or wider, within the bound.
No kernel may reach another device: no remote copies, remote signals or barrier semaphores. Data moves between devices by JAX's collectives and lax.ppermute only.
A program may use at most 128 MiB of HBM per device.

v0:
```python
import jax
import jax.numpy as jnp
from jax import lax
from jax.sharding import PartitionSpec as P


def shifted(value, axis, steps):
    count = lax.axis_size(axis)
    pairs = [(source, (source + steps) % count) for source in range(count)]
    return lax.ppermute(value, axis, pairs)


def slot_tables(chosen_ids, experts, capacity):
    tok_count, chosen = chosen_ids.shape
    flat_ids = chosen_ids.reshape(-1)
    columns = jnp.arange(experts, dtype=jnp.int32)
    onehot = (flat_ids[:, None] == columns[None, :]).astype(jnp.int32)
    earlier = jnp.cumsum(onehot, axis=0) - onehot
    slot_rank = jnp.sum(earlier * onehot, axis=1)
    kept_pair = (flat_ids < experts) & (slot_rank < capacity)
    slot_index = jnp.where(kept_pair, flat_ids * capacity + slot_rank, experts * capacity)
    slot_rows = jnp.arange(experts * capacity, dtype=jnp.int32)
    placed = slot_index[None, :] == slot_rows[:, None]
    pair_index = jnp.arange(tok_count * chosen, dtype=jnp.int32)
    source_pair = jnp.sum(jnp.where(placed, pair_index[None, :], 0), axis=1)
    filled = jnp.any(placed, axis=1)
    return (slot_index, source_pair, filled)


def shards(block_input, output_grad, expert_ids, gate_weights, gate_proj, up_proj, down_proj):
    acts_local = block_input[0]
    grad_local = output_grad[0]
    chosen_ids = expert_ids[0]
    route_weight = gate_weights[0]
    tok_count, chosen = chosen_ids.shape
    width = acts_local.shape[1]
    local_count = gate_proj.shape[1]
    dp_count = lax.axis_size("dp")
    expert_count = lax.axis_size("expert")
    experts = local_count * expert_count
    capacity = tok_count // 16
    slot_index, source_pair, filled = slot_tables(chosen_ids, experts, capacity)
    source_token = source_pair // chosen
    slot_weight = route_weight.reshape(-1)[source_pair]
    send_acts = jnp.where(filled[:, None], acts_local[source_token], jnp.zeros((), jnp.bfloat16))
    scaled = slot_weight[:, None] * grad_local[source_token].astype(jnp.float32)
    send_grad = jnp.where(filled[:, None], scaled, 0.0).astype(jnp.bfloat16)
    send_acts = send_acts.reshape(experts, capacity, width)
    send_grad = send_grad.reshape(experts, capacity, width)
    acts_copies = jnp.broadcast_to(send_acts[None], (dp_count,) + send_acts.shape).reshape(
        dp_count * experts, capacity, width
    )
    grad_copies = jnp.broadcast_to(send_grad[None], (dp_count,) + send_grad.shape).reshape(
        dp_count * experts, capacity, width
    )
    recv_acts, recv_grad = (
        lax.all_to_all(acts_copies, ("dp", "expert"), split_axis=0, concat_axis=1, tiled=True),
        lax.all_to_all(grad_copies, ("dp", "expert"), split_axis=0, concat_axis=1, tiled=True),
    )
    gate_local = gate_proj[0]
    upper_local = up_proj[0]
    lower_local = down_proj[0]
    gate_pre = jnp.einsum("erd,edh->erh", recv_acts, gate_local, preferred_element_type=jnp.float32)
    up_value = jnp.einsum(
        "erd,edh->erh", recv_acts, upper_local, preferred_element_type=jnp.float32
    )
    grad_hidden = jnp.einsum(
        "erd,ehd->erh", recv_grad, lower_local, preferred_element_type=jnp.float32
    )
    sigma_gate = jax.nn.sigmoid(gate_pre)
    swish = gate_pre * sigma_gate
    hidden = swish * up_value
    scores = jnp.sum(hidden * grad_hidden, axis=2)
    lower_grad = jnp.einsum(
        "erh,erd->ehd", hidden.astype(jnp.bfloat16), recv_grad, preferred_element_type=jnp.float32
    ).astype(jnp.bfloat16)
    delta_gate = (
        grad_hidden * up_value * sigma_gate * (1.0 + gate_pre * (1.0 - sigma_gate))
    ).astype(jnp.bfloat16)
    delta_up = (grad_hidden * swish).astype(jnp.bfloat16)
    gate_grad = jnp.einsum(
        "erd,erh->edh", recv_acts, delta_gate, preferred_element_type=jnp.float32
    ).astype(jnp.bfloat16)
    upper_grad = jnp.einsum(
        "erd,erh->edh", recv_acts, delta_up, preferred_element_type=jnp.float32
    ).astype(jnp.bfloat16)
    partial_value = jnp.einsum(
        "erh,edh->erd", delta_gate, gate_local, preferred_element_type=jnp.float32
    ) + jnp.einsum("erh,edh->erd", delta_up, upper_local, preferred_element_type=jnp.float32)
    back_rows, back_scores = (
        lax.all_to_all(partial_value, ("dp", "expert"), split_axis=1, concat_axis=0, tiled=True),
        lax.all_to_all(scores, ("dp", "expert"), split_axis=1, concat_axis=0, tiled=True),
    )
    slot_grad = jnp.sum(back_rows.reshape(dp_count, experts * capacity, width), axis=0).astype(
        jnp.bfloat16
    )
    slot_scores = jnp.sum(back_scores.reshape(dp_count, experts * capacity), axis=0)
    token_rows = jnp.arange(tok_count, dtype=jnp.int32)
    token_map = ((source_token[:, None] == token_rows[None, :]) & filled[:, None]).astype(
        jnp.bfloat16
    )
    input_grad = jnp.einsum(
        "st,sd->td", token_map, slot_grad, preferred_element_type=jnp.float32
    ).astype(jnp.bfloat16)
    padded_scores = jnp.concatenate([slot_scores, jnp.zeros((1,), jnp.float32)])
    weight_grad = (padded_scores[slot_index] / route_weight.reshape(-1)).reshape(tok_count, chosen)
    received = shifted(input_grad, "pipe", -1)
    return (received[None], weight_grad[None], gate_grad[None], upper_grad[None], lower_grad[None])


def solution(mesh):
    in_specs = (
        P("pipe", ("dp", "expert"), None),
        P("pipe", ("dp", "expert"), None),
        P("pipe", ("dp", "expert"), None),
        P("pipe", ("dp", "expert"), None),
        P("pipe", "expert", None, "dp"),
        P("pipe", "expert", None, "dp"),
        P("pipe", "expert", "dp", None),
    )
    out_specs = (
        P("pipe", ("dp", "expert"), None),
        P("pipe", ("dp", "expert"), None),
        P("pipe", "expert", None, "dp"),
        P("pipe", "expert", None, "dp"),
        P("pipe", "expert", "dp", None),
    )
    return jax.shard_map(shards, mesh=mesh, in_specs=in_specs, out_specs=out_specs, check_vma=False)
```

profile of v0, /device:TPU:0, one launch (start us, length us, event | category | flops | bytes accessed | tf_op | source)
XLA Modules:
  0.0 79.5 jit_solution(6049653979190262560)
XLA Ops:
  0.6 0.0 copy-start
  0.6 0.0 copy-start.9
  0.7 0.9 %copy.28 = s32[1,128,6]{2,1,0:T(8,128)S(1)} copy(s32[1,128,6]{1,0,2:T(1,128)} %param.9) | data formatting | bytes 6144 | tf_op args[2]
  1.6 0.1 reshape_squeeze.7
  1.7 0.1 eq.52
  1.9 0.6 reduce-window.6
  2.4 0.2 slice_reduce_fusion
  2.7 0.2 reduce-window.9
  2.8 0.1 add_bitcast_fusion
  3.0 0.1 fusion.23
  3.1 0.1 select_reduce_fusion
  3.2 0.1 broadcast_in_dim.81
  3.3 1.9 %gather_fusion.2 = bf16[16,3072]{1,0:T(8,128)(2,1)S(1)} fusion(bf16[128,3072]{1,0:T(8,128)(2,1)} %bitcast.109, s32[1024]{0:T(1024)S(1)} %get-tuple-element.53), kind=kCustom, calls=%fused_computation.2 | custom fusion | bytes 196672 | tf_op jit(solution)/shard_map/gather | solution.py:45
  5.3 0.1 bitcast_select_fusion
  5.4 0.8 broadcast_in_dim.86
  6.1 5.2 %all-to-all-start.1 = ((bf16[8,8,3072]{2,1,0:T(8,128)(2,1)}), bf16[8,8,3072]{2,1,0:T(8,128)(2,1)S(1)}, u32[]{:S(2)}, u32[]{:S(2)}) async-start(bf16[8,8,3072]{2,1,0:T(8,128)(2,1)} %bitcast.11), calls=%async_computation.1 | async-start | bytes 786432 | tf_op jit(solution)/shard_map/all_to_all | solution.py:57
  11.3 0.1 copy.32
  11.5 0.1 lt.81
  11.7 0.1 copy.30
  11.8 0.1 reshape_squeeze.8
  11.9 0.6 gather_fusion
  12.5 0.1 mul.70
  12.6 0.6 gather_fusion.1
  13.3 0.7 fusion.20
  14.0 4.7 %all-to-all-done.1 = bf16[8,8,3072]{2,1,0:T(8,128)(2,1)S(1)} async-done(((bf16[8,8,3072]{2,1,0:T(8,128)(2,1)}), bf16[8,8,3072]{2,1,0:T(8,128)(2,1)S(1)}, u32[]{:S(2)}, u32[]{:S(2)}) %all-to-all-start.1) | async-done | bytes 393248 | tf_op jit(solution)/shard_map/all_to_all | solution.py:57
  18.7 1.7 %broadcast_in_dim.84 = bf16[4,2,8,3072]{3,2,1,0:T(8,128)(2,1)} broadcast(bf16[2,8,3072]{2,1,0:T(8,128)(2,1)} %fusion.20), dimensions={1,2,3} | broadcast | bytes 491520 | tf_op jit(solution)/shard_map/broadcast_in_dim | solution.py:53
  20.4 4.1 %all-to-all-start = ((bf16[8,8,3072]{2,1,0:T(8,128)(2,1)}), bf16[8,8,3072]{2,1,0:T(8,128)(2,1)}, u32[]{:S(2)}, u32[]{:S(2)}) async-start(bf16[8,8,3072]{2,1,0:T(8,128)(2,1)} %bitcast.108), calls=%async_computation | async-start | bytes 786432 | tf_op jit(solution)/shard_map/all_to_all | solution.py:58
  24.5 1.0 %fusion.6 = f32[64,256]{1,0:T(8,128)} fusion(bf16[1,1,3072,256]{3,2,1,0:T(8,128)(2,1)S(1)} %copy-done, bf16[8,8,3072]{2,1,0:T(8,128)(2,1)S(1)} %all-to-all-done.1), kind=kOutput, calls=%fused_computation.14 | convolution fusion | flops 100663296 | bytes 2031616 | tf_op jit(solution)/shard_map/erd,edh->erh/dot_general | solution.py:63
  25.5 1.0 %fusion.9 = f32[64,256]{1,0:T(8,128)} fusion(bf16[1,1,3072,256]{3,2,1,0:T(8,128)(2,1)S(1)} %copy-done.1, bf16[8,8,3072]{2,1,0:T(8,128)(2,1)S(1)} %all-to-all-done.1), kind=kOutput, calls=%fused_computation.17 | convolution fusion | flops 100663296 | bytes 2031616 | tf_op jit(solution)/shard_map/erd,edh->erh/dot_general | solution.py:64
  26.5 5.4 %all-to-all-done = bf16[8,8,3072]{2,1,0:T(8,128)(2,1)} async-done(((bf16[8,8,3072]{2,1,0:T(8,128)(2,1)}), bf16[8,8,3072]{2,1,0:T(8,128)(2,1)}, u32[]{:S(2)}, u32[]{:S(2)}) %all-to-all-start) | async-done | bytes 393248 | tf_op jit(solution)/shard_map/all_to_all | solution.py:58
  31.9 2.7 %multiply_reduce_fusion = (f32[64]{0:T(128)}, bf16[64,256]{1,0:T(8,128)(2,1)S(1)}, bf16[64,256]{1,0:T(8,128)(2,1)S(1)}) fusion(f32[64,256]{1,0:T(8,128)} %fusion.9, f32[64,256]{1,0:T(8,128)} %fusion.6, bf16[1,1,256,3072]{3,2,1,0:T(8,128)(2,1)} %param.13, bf16[8,8,3072]{2,1,0:T(8,128)(2,1)} %all-to-all-done), kind=kOutput, calls=%fused_computation.32 | convolution fusion | flops 100925376 | bytes 2162944 | tf_op jit(solution)/shard_map/erd,ehd->erh/dot_general | solution.py:67
  34.6 0.6 fusion.4
  35.2 0.0 copy-done.6
  35.2 0.0 copy-done.7
  35.3 0.6 fusion.3
  35.9 0.0 copy-start.12
  35.9 0.0 copy-start.8
  35.9 1.7 %copy.31 = f32[1,64,3072]{2,0,1:T(1,128)} copy(f32[1,64,3072]{2,1,0:T(8,128)S(1)} %fusion.3) | data formatting | bytes 1572864 | tf_op jit(solution)/shard_map/add | solution.py:87
  37.6 3.7 %all-to-all-start.2 = ((f32[1,64,3072]{2,0,1:T(1,128)}), f32[1,64,3072]{2,0,1:T(1,128)S(1)}, u32[]{:S(2)}, u32[]{:S(2)}) async-start(f32[1,64,3072]{2,0,1:T(1,128)} %copy.31), calls=%async_computation.2 | async-start | bytes 1572864 | tf_op jit(solution)/shard_map/all_to_all | solution.py:91
  41.3 0.1 copy.33
  41.4 0.1 mul.82
  41.5 0.6 and_select_fusion.2
  42.2 0.7 all_to_all.14
  42.8 1.7 %fusion.1 = bf16[1,1,3072,256]{3,2,1,0:T(8,128)(2,1)} fusion(bf16[64,256]{1,0:T(8,128)(2,1)S(1)} %copy-done.8, bf16[8,8,3072]{2,1,0:T(8,128)(2,1)S(1)} %all-to-all-done.1), kind=kOutput, calls=%fused_computation.7 | convolution fusion | flops 101449728 | bytes 1998848 | tf_op jit(solution)/shard_map/erd,erh->edh/dot_general | solution.py:84
  44.6 2.7 %fusion.2 = bf16[1,1,256,3072]{3,2,1,0:T(8,128)(2,1)} fusion(bf16[8,8,3072]{2,1,0:T(8,128)(2,1)} %all-to-all-done, f32[64,256]{1,0:T(8,128)S(1)} %copy-done.4, f32[64,256]{1,0:T(8,128)S(1)} %copy-done.3), kind=kOutput, calls=%fused_computation.8 | convolution fusion | flops 101548032 | bytes 2097152 | tf_op jit(solution)/shard_map/erh,erd->ehd/dot_general | solution.py:74
  47.3 5.6 %all-to-all-done.2 = f32[1,64,3072]{2,0,1:T(1,128)S(1)} async-done(((f32[1,64,3072]{2,0,1:T(1,128)}), f32[1,64,3072]{2,0,1:T(1,128)S(1)}, u32[]{:S(2)}, u32[]{:S(2)}) %all-to-all-start.2) | async-done | bytes 786464 | tf_op jit(solution)/shard_map/all_to_all | solution.py:91
  52.9 3.3 %all-to-all-start.3 = ((f32[1,8,8]{2,0,1:T(1,128)}), f32[1,8,8]{2,0,1:T(1,128)S(1)}, u32[]{:S(2)}, u32[]{:S(2)}) async-start(f32[1,8,8]{2,0,1:T(1,128)} %bitcast.17), calls=%async_computation.3 | async-start | bytes 8192 | tf_op jit(solution)/shard_map/all_to_all | solution.py:92
  56.2 0.1 copy.37
  56.4 1.2 %convolution_convert_fusion.3 = bf16[128,3072]{1,0:T(8,128)(2,1)S(1)} fusion(bf16[16,3072]{1,0:T(8,128)(2,1)S(1)} %reduce_sum.52, s32[16]{0:T(128)} %and_select_fusion.2, pred[16]{0:T(512)(128)(4,1)} %copy-done.11), kind=kOutput, calls=%fused_computation.9 | convolution fusion | flops 12980224 | bytes 884816 | tf_op jit(solution)/shard_map/st,sd->td/dot_general | solution.py:102
  57.6 3.7 %collective-permute-start = (bf16[128,3072]{1,0:T(8,128)(2,1)S(1)}, bf16[128,3072]{1,0:T(8,128)(2,1)S(1)}, u32[]{:S(2)}, u32[]{:S(2)}) collective-permute-start(bf16[128,3072]{1,0:T(8,128)(2,1)S(1)} %convolution_convert_fusion.3), channel_id=1, source_target_pairs={{0,24},{8,0},{16,8},{24,16},{1,25},{9,1},{17,9},{25,17},{2,26},{10... | collective-permute-start | bytes 2359304 | tf_op jit(solution)/shard_map/ppermute | solution.py:10
  61.2 2.5 %fusion = bf16[1,1,3072,256]{3,2,1,0:T(8,128)(2,1)} fusion(bf16[64,256]{1,0:T(8,128)(2,1)} %copy-done.6, bf16[8,8,3072]{2,1,0:T(8,128)(2,1)S(1)} %all-to-all-done.1), kind=kOutput, calls=%fused_computation.6 | convolution fusion | flops 101449728 | bytes 1998848 | tf_op jit(solution)/shard_map/erd,erh->edh/dot_general | solution.py:81
  63.7 0.0 all-to-all-done.3
  63.7 0.5 broadcast.371
  64.2 0.7 reduce.29
  64.9 0.1 reshape.293
  65.0 0.7 fusion.38
  65.7 4.4 %fusion.34 = (f32[768]{0:T(1024)S(1)}, s32[768,1]{0,1:T(1,128)S(1)}) fusion(f32[]{:T(128)} %bitcast.27, f32[]{:T(128)} %bitcast.28, f32[]{:T(128)} %bitcast.29, f32[]{:T(128)} %bitcast.30, f32[]{:T(128)} %bitcast.31, f32[]{:T(128)} %bitcast.33, f32[]{:T(128)} %bitcast.32, s32[768,1]{0,1:T(1,128)S(1)} %mul.82, pred[768,1]{0,1:T(4,128)(4,1)S(1)} %lt.81, ...), kind=kLoop, calls=%fused_computation.76 | loop fusion | flops 14592 | bytes 13084 | tf_op jit(solution)/shard_map/gather | solution.py:106
  70.1 0.1 compare_reduce_fusion.9
  70.2 5.6 %select_select_fusion = f32[768]{0:T(1024)S(1)} fusion(pred[768]{0:T(1024)(128)(4,1)S(1)} %get-tuple-element.29, pred[768]{0:T(1024)(128)(4,1)S(1)} %get-tuple-element.28, pred[768]{0:T(1024)(128)(4,1)S(1)} %get-tuple-element.27, pred[768]{0:T(1024)(128)(4,1)S(1)} %get-tuple-element.26, pred[768]{0:T(1024)(128)(4,1)S(1)} %get-tuple-element.25, ...), kind=kLoop, calls=%fused_computation.72 | loop fusion | flops 7680 | bytes 13860 | tf_op jit(solution)/shard_map/gather | solution.py:106
  75.9 0.1 gather.21
  76.0 0.9 %div.29 = f32[1,128,6]{2,1,0:T(8,128)S(1)} divide(f32[1,128,6]{2,1,0:T(8,128)S(1)} %gather.21, f32[1,128,6]{2,1,0:T(8,128)} %copy-done.5) | non-fusion elementwise | flops 768 | bytes 9216 | tf_op jit(solution)/shard_map/div | solution.py:106
  76.9 0.7 copy.36
  77.5 1.0 %collective-permute-done = bf16[128,3072]{1,0:T(8,128)(2,1)S(1)} collective-permute-done((bf16[128,3072]{1,0:T(8,128)(2,1)S(1)}, bf16[128,3072]{1,0:T(8,128)(2,1)S(1)}, u32[]{:S(2)}, u32[]{:S(2)}) %collective-permute-start) | collective-permute-done | bytes 786464 | tf_op jit(solution)/shard_map/ppermute | solution.py:10
  78.6 0.9 %copy.41 = bf16[1,128,3072]{2,1,0:T(8,128)(2,1)} copy(bf16[1,128,3072]{2,1,0:T(8,128)(2,1)S(1)} %bitcast.111) | data formatting | bytes 1572864
  (33 shorter events, 0.2 us)
Async XLA Ops:
  0.6 23.9 %copy-start = (bf16[1,1,3072,256]{3,2,1,0:T(8,128)(2,1)S(1)}, bf16[1,1,3072,256]{3,2,1,0:T(8,128)(2,1)}, u32[]{:S(2)}) copy-start(bf16[1,1,3072,256]{3,2,1,0:T(8,128)(2,1)} %param.11) | copy-start | bytes 4718596
  0.6 10.7 %copy-start.9 = (s32[1,128,6]{1,0,2:T(1,128)S(1)}, s32[1,128,6]{1,0,2:T(1,128)}, u32[]{:S(2)}) copy-start(s32[1,128,6]{1,0,2:T(1,128)} %param.9) | copy-start | bytes 9220
  0.7 11.0 %copy-start.10 = (f32[1,128,6]{1,0,2:T(1,128)S(1)}, f32[1,128,6]{1,0,2:T(1,128)}, u32[]{:S(2)}) copy-start(f32[1,128,6]{1,0,2:T(1,128)} %param.10) | copy-start | bytes 9220
  2.8 9.8 %copy-start.2 = (bf16[1,128,3072]{2,1,0:T(8,128)(2,1)S(1)}, bf16[1,128,3072]{2,1,0:T(8,128)(2,1)}, u32[]{:S(2)}) copy-start(bf16[1,128,3072]{2,1,0:T(8,128)(2,1)} %param.8) | copy-start | bytes 2359300
  3.1 9.5 %copy-start.11 = (pred[16]{0:T(512)(128)(4,1)}, pred[16]{0:T(512)(128)(4,1)S(1)}, u32[]{:S(2)}) copy-start(pred[16]{0:T(512)(128)(4,1)S(1)} %fusion.23) | copy-start | bytes 52
  3.2 9.4 %copy-start.13 = (s32[16]{0:T(128)}, s32[16]{0:T(128)S(1)}, u32[]{:S(2)}) copy-start(s32[16]{0:T(128)S(1)} %select_reduce_fusion) | copy-start | bytes 196
  6.1 12.6 %all-to-all-start.1 = ((bf16[8,8,3072]{2,1,0:T(8,128)(2,1)}), bf16[8,8,3072]{2,1,0:T(8,128)(2,1)S(1)}, u32[]{:S(2)}, u32[]{:S(2)}) async-start(bf16[8,8,3072]{2,1,0:T(8,128)(2,1)} %bitcast.11), calls=%async_computation.1 | async-start | bytes 786432 | tf_op jit(solution)/shard_map/all_to_all | solution.py:57
  11.8 1.5 %copy-start.5 = (f32[1,128,6]{2,1,0:T(8,128)}, f32[1,128,6]{2,1,0:T(8,128)S(1)}, u32[]{:S(2)}) copy-start(f32[1,128,6]{2,1,0:T(8,128)S(1)} %copy.30) | copy-start | bytes 9220
  14.0 11.5 %copy-start.1 = (bf16[1,1,3072,256]{3,2,1,0:T(8,128)(2,1)S(1)}, bf16[1,1,3072,256]{3,2,1,0:T(8,128)(2,1)}, u32[]{:S(2)}) copy-start(bf16[1,1,3072,256]{3,2,1,0:T(8,128)(2,1)} %param.12) | copy-start | bytes 4718596
  20.4 11.5 %all-to-all-start = ((bf16[8,8,3072]{2,1,0:T(8,128)(2,1)}), bf16[8,8,3072]{2,1,0:T(8,128)(2,1)}, u32[]{:S(2)}, u32[]{:S(2)}) async-start(bf16[8,8,3072]{2,1,0:T(8,128)(2,1)} %bitcast.108), calls=%async_computation | async-start | bytes 786432 | tf_op jit(solution)/shard_map/all_to_all | solution.py:58
  34.6 0.6 copy-start.6
  34.6 0.6 copy-start.7
  35.9 5.7 %copy-start.14 = (s32[16]{0:T(128)S(1)}, s32[16]{0:T(128)}, u32[]{:S(2)}) copy-start(s32[16]{0:T(128)} %copy-done.13) | copy-start | bytes 196
  35.9 6.3 %copy-start.12 = (f32[64]{0:T(128)S(1)}, f32[64]{0:T(128)}, u32[]{:S(2)}) copy-start(f32[64]{0:T(128)} %get-tuple-element.32) | copy-start | bytes 772
  35.9 7.0 %copy-start.8 = (bf16[64,256]{1,0:T(8,128)(2,1)S(1)}, bf16[64,256]{1,0:T(8,128)(2,1)}, u32[]{:S(2)}) copy-start(bf16[64,256]{1,0:T(8,128)(2,1)} %copy-done.7) | copy-start | bytes 98308
  37.6 7.0 %copy-start.3 = (f32[64,256]{1,0:T(8,128)S(1)}, f32[64,256]{1,0:T(8,128)}, u32[]{:S(2)}) copy-start(f32[64,256]{1,0:T(8,128)} %fusion.6) | copy-start | bytes 196612
  37.6 7.0 %copy-start.4 = (f32[64,256]{1,0:T(8,128)S(1)}, f32[64,256]{1,0:T(8,128)}, u32[]{:S(2)}) copy-start(f32[64,256]{1,0:T(8,128)} %fusion.9) | copy-start | bytes 196612
  37.6 15.3 %all-to-all-start.2 = ((f32[1,64,3072]{2,0,1:T(1,128)}), f32[1,64,3072]{2,0,1:T(1,128)S(1)}, u32[]{:S(2)}, u32[]{:S(2)}) async-start(f32[1,64,3072]{2,0,1:T(1,128)} %copy.31), calls=%async_computation.2 | async-start | bytes 1572864 | tf_op jit(solution)/shard_map/all_to_all | solution.py:91
  52.9 10.8 %all-to-all-start.3 = ((f32[1,8,8]{2,0,1:T(1,128)}), f32[1,8,8]{2,0,1:T(1,128)S(1)}, u32[]{:S(2)}, u32[]{:S(2)}) async-start(f32[1,8,8]{2,0,1:T(1,128)} %bitcast.17), calls=%async_computation.3 | async-start | bytes 8192 | tf_op jit(solution)/shard_map/all_to_all | solution.py:92
  57.6 21.0 %collective-permute-start = (bf16[128,3072]{1,0:T(8,128)(2,1)S(1)}, bf16[128,3072]{1,0:T(8,128)(2,1)S(1)}, u32[]{:S(2)}, u32[]{:S(2)}) collective-permute-start(bf16[128,3072]{1,0:T(8,128)(2,1)S(1)} %convolution_convert_fusion.3), channel_id=1, source_target_pairs={{0,24},{8,0},{16,8},{24,16},{1,25},{9,1},{17,9},{25,17},{2,26},{10... | collective-permute-start | bytes 2359304 | tf_op jit(solution)/shard_map/ppermute | solution.py:10
where the time goes:
time: 80.3 us; the launch traced here: 79.5 us
  starting transfers between devices  19.9 us (25%)
  waiting for transfers between devices  16.7 us (21%)
  other arithmetic  14.3 us (18%)
  matrix products  14.1 us (18%)
  local copies, waits for them, and re-layouts  13.5 us (17%)
  between operations  0.92 us (1%)
    gather x3, other arithmetic, shards(): padded_scores[slot_index] / route_weight.reshape(-1)  10.2 us
    all_to_all x1, waiting for transfers between devices, shards(): lax.all_to_all(partial_value, ('dp', 'expert'), split_axis=1, concat_axis...  5.58 us
    all_to_all x1, waiting for transfers between devices, shards(): lax.all_to_all(grad_copies, ('dp', 'expert'), split_axis=0, concat_axis=1...  5.38 us
    all_to_all x1, starting transfers between devices, shards(): lax.all_to_all(acts_copies, ('dp', 'expert'), split_axis=0, concat_axis=1...  5.2 us
    all_to_all x1, waiting for transfers between devices, shards(): lax.all_to_all(acts_copies, ('dp', 'expert'), split_axis=0, concat_axis=1...  4.73 us
    all_to_all x1, starting transfers between devices, shards(): lax.all_to_all(grad_copies, ('dp', 'expert'), split_axis=0, concat_axis=1...  4.1 us
    all_to_all x1, starting transfers between devices, shards(): lax.all_to_all(partial_value, ('dp', 'expert'), split_axis=1, concat_axis...  3.68 us
    ppermute x1, starting transfers between devices, shifted(): return lax.ppermute(value, axis, pairs)  3.66 us
  transfers between devices with their start and end apart: 5, of which 4 were waited for; matrix products, arithmetic and copies ran while one was open for 35% of the time, Pallas kernels for 0%

commit v1 on v0

--- a/solution.py
+++ b/solution.py
@@ -2,6 +2,12 @@
 import jax.numpy as jnp
 from jax import lax
 from jax.sharding import PartitionSpec as P
+
+
+def trade_parts(x, name, split, join):
+    pieces = jnp.split(x, lax.axis_size(name), axis=split)
+    received = lax.all_to_all(jnp.stack(pieces), name, 0, 0)
+    return jnp.concatenate(received, axis=join)
 
 
 def shifted(value, axis, steps):
@@ -54,7 +60,7 @@
         dp_count * experts, capacity, width
     )
     recv_acts, recv_grad = (
-        lax.all_to_all(acts_copies, ("dp", "expert"), split_axis=0, concat_axis=1, tiled=True),
+        trade_parts(acts_copies, ("dp", "expert"), 0, 1),
         lax.all_to_all(grad_copies, ("dp", "expert"), split_axis=0, concat_axis=1, tiled=True),
     )
     gate_local = gate_proj[0]

time: 80.3 us -> 85 us (1.059)
  local copies, waits for them, and re-layouts: 13.5 us -> 18.2 us
    unnamed x35 -> x42, local copies, waits for them, and re-layouts: 2.79 us -> 7.57 us
  transfers between devices with their start and end apart: 5 -> 5, of which waited for: 4 -> 4; matrix products, arithmetic and copies ran while one was open for 35% -> 33% of each run, Pallas kernels for 0% -> 0%
where the time goes in v1:
time: 85 us; the launch traced here: 84.2 us
  starting transfers between devices  19.9 us (23%)
  local copies, waits for them, and re-layouts  18.2 us (21%)
  waiting for transfers between devices  16.7 us (20%)
  other arithmetic  14.3 us (17%)
  matrix products  14.1 us (17%)
  between operations  0.91 us (1%)
    gather x3, other arithmetic, shards(): padded_scores[slot_index] / route_weight.reshape(-1)  10.2 us
    unnamed x42, local copies, waits for them, and re-layouts  7.57 us
    all_to_all x1, waiting for transfers between devices, shards(): lax.all_to_all(partial_value, ('dp', 'expert'), split_axis=1, concat_axis...  5.58 us
    all_to_all x1, waiting for transfers between devices, shards(): lax.all_to_all(grad_copies, ('dp', 'expert'), split_axis=0, concat_axis=1...  5.38 us
    all_to_all x1, starting transfers between devices, trade_parts(): received = lax.all_to_all(jnp.stack(pieces), name, 0, 0)  5.2 us
    all_to_all x1, waiting for transfers between devices, trade_parts(): received = lax.all_to_all(jnp.stack(pieces), name, 0, 0)  4.74 us
    all_to_all x1, starting transfers between devices, shards(): lax.all_to_all(grad_copies, ('dp', 'expert'), split_axis=0, concat_axis=1...  4.1 us
    all_to_all x1, starting transfers between devices, shards(): lax.all_to_all(partial_value, ('dp', 'expert'), split_axis=1, concat_axis...  3.68 us
  transfers between devices with their start and end apart: 5, of which 4 were waited for; matrix products, arithmetic and copies ran while one was open for 33% of the time, Pallas kernels for 0%

profile of v1, /device:TPU:0, one launch (start us, length us, event | category | flops | bytes accessed | tf_op | source)
XLA Modules:
  0.0 84.2 jit_solution(5291984473666100653)
XLA Ops:
  0.6 0.9 %copy.28 = s32[1,128,6]{2,1,0:T(8,128)S(1)} copy(s32[1,128,6]{1,0,2:T(1,128)} %param.9) | data formatting | bytes 6144 | tf_op args[2]
  1.6 0.1 reshape_squeeze.7
  1.7 0.1 eq.52
  1.8 0.6 reduce-window.6
  2.4 0.2 slice_reduce_fusion
  2.6 0.2 reduce-window.9
  2.9 0.1 fusion.31
  3.1 0.1 select_reduce_fusion
  3.2 0.1 broadcast_in_dim.81
  3.3 0.3 copy-done.11
  3.6 0.1 copy-done.13
  3.7 2.0 %gather_fusion.2 = bf16[16,3072]{1,0:T(8,128)(2,1)S(1)} fusion(bf16[128,3072]{1,0:T(8,128)(2,1)} %bitcast.149, s32[1024]{0:T(1024)S(1)} %get-tuple-element.53), kind=kCustom, calls=%fused_computation.2 | custom fusion | bytes 196672 | tf_op jit(solution)/shard_map/gather | solution.py:51
  5.7 0.1 bitcast_select_fusion
  5.8 0.6 fusion.30
  6.5 0.6 fusion.29
  7.1 0.6 fusion.28
  7.7 0.6 fusion.27
  8.3 0.6 fusion.26
  8.9 0.6 fusion.25
  9.6 0.6 fusion.24
  10.2 0.6 fusion.23
  10.8 5.2 %all-to-all-start.1 = ((bf16[8,1,8,3072]{3,2,1,0:T(8,128)(2,1)}), bf16[8,1,8,3072]{3,2,1,0:T(8,128)(2,1)S(1)}, u32[]{:S(2)}, u32[]{:S(2)}) async-start(bf16[8,1,8,3072]{3,2,1,0:T(8,128)(2,1)} %fusion.23), calls=%async_computation.1 | async-start | bytes 786432 | tf_op jit(solution)/shard_map/all_to_all | solution.py:9
  16.0 0.1 copy.32
  16.2 0.1 lt.81
  16.3 0.1 copy.30
  16.5 0.1 reshape_squeeze.8
  16.6 0.6 gather_fusion
  17.2 0.1 mul.70
  17.3 0.6 gather_fusion.1
  18.0 0.7 fusion.20
  18.7 4.7 %all-to-all-done.1 = bf16[8,1,8,3072]{3,2,1,0:T(8,128)(2,1)S(1)} async-done(((bf16[8,1,8,3072]{3,2,1,0:T(8,128)(2,1)}), bf16[8,1,8,3072]{3,2,1,0:T(8,128)(2,1)S(1)}, u32[]{:S(2)}, u32[]{:S(2)}) %all-to-all-start.1) | async-done | bytes 393248 | tf_op jit(solution)/shard_map/all_to_all | solution.py:9
  23.4 1.7 %broadcast_in_dim.84 = bf16[4,2,8,3072]{3,2,1,0:T(8,128)(2,1)} broadcast(bf16[2,8,3072]{2,1,0:T(8,128)(2,1)} %fusion.20), dimensions={1,2,3} | broadcast | bytes 491520 | tf_op jit(solution)/shard_map/broadcast_in_dim | solution.py:59
  25.1 4.1 %all-to-all-start = ((bf16[8,8,3072]{2,1,0:T(8,128)(2,1)}), bf16[8,8,3072]{2,1,0:T(8,128)(2,1)}, u32[]{:S(2)}, u32[]{:S(2)}) async-start(bf16[8,8,3072]{2,1,0:T(8,128)(2,1)} %bitcast.148), calls=%async_computation | async-start | bytes 786432 | tf_op jit(solution)/shard_map/all_to_all | solution.py:64
  29.2 1.0 %fusion.6 = f32[64,256]{1,0:T(8,128)} fusion(bf16[1,1,3072,256]{3,2,1,0:T(8,128)(2,1)S(1)} %copy-done, bf16[8,1,8,3072]{3,2,1,0:T(8,128)(2,1)S(1)} %all-to-all-done.1), kind=kOutput, calls=%fused_computation.14 | convolution fusion | flops 100663296 | bytes 2031616 | tf_op jit(solution)/shard_map/erd,edh->erh/dot_general | solution.py:69
  30.2 1.0 %fusion.9 = f32[64,256]{1,0:T(8,128)} fusion(bf16[1,1,3072,256]{3,2,1,0:T(8,128)(2,1)S(1)} %copy-done.1, bf16[8,1,8,3072]{3,2,1,0:T(8,128)(2,1)S(1)} %all-to-all-done.1), kind=kOutput, calls=%fused_computation.17 | convolution fusion | flops 100663296 | bytes 2031616 | tf_op jit(solution)/shard_map/erd,edh->erh/dot_general | solution.py:70
  31.2 5.4 %all-to-all-done = bf16[8,8,3072]{2,1,0:T(8,128)(2,1)} async-done(((bf16[8,8,3072]{2,1,0:T(8,128)(2,1)}), bf16[8,8,3072]{2,1,0:T(8,128)(2,1)}, u32[]{:S(2)}, u32[]{:S(2)}) %all-to-all-start) | async-done | bytes 393248 | tf_op jit(solution)/shard_map/all_to_all | solution.py:64
  36.6 2.7 %multiply_reduce_fusion = (f32[64]{0:T(128)}, bf16[64,256]{1,0:T(8,128)(2,1)S(1)}, bf16[64,256]{1,0:T(8,128)(2,1)S(1)}) fusion(f32[64,256]{1,0:T(8,128)} %fusion.9, f32[64,256]{1,0:T(8,128)} %fusion.6, bf16[1,1,256,3072]{3,2,1,0:T(8,128)(2,1)} %param.13, bf16[8,8,3072]{2,1,0:T(8,128)(2,1)} %all-to-all-done), kind=kOutput, calls=%fused_computation.32 | convolution fusion | flops 100925376 | bytes 2162944 | tf_op jit(solution)/shard_map/erd,ehd->erh/dot_general | solution.py:73
  39.3 0.6 fusion.4
  40.0 0.6 fusion.3
  40.6 1.7 %copy.31 = f32[1,64,3072]{2,0,1:T(1,128)} copy(f32[1,64,3072]{2,1,0:T(8,128)S(1)} %fusion.3) | data formatting | bytes 1572864 | tf_op jit(solution)/shard_map/add | solution.py:93
  42.3 3.7 %all-to-all-start.2 = ((f32[1,64,3072]{2,0,1:T(1,128)}), f32[1,64,3072]{2,0,1:T(1,128)S(1)}, u32[]{:S(2)}, u32[]{:S(2)}) async-start(f32[1,64,3072]{2,0,1:T(1,128)} %copy.31), calls=%async_computation.2 | async-start | bytes 1572864 | tf_op jit(solution)/shard_map/all_to_all | solution.py:97
  46.0 0.1 copy.33
  46.1 0.1 mul.82
  46.2 0.6 and_select_fusion.2
  46.8 0.7 all_to_all.14
  47.5 1.7 %fusion.1 = bf16[1,1,3072,256]{3,2,1,0:T(8,128)(2,1)} fusion(bf16[64,256]{1,0:T(8,128)(2,1)S(1)} %copy-done.8, bf16[8,1,8,3072]{3,2,1,0:T(8,128)(2,1)S(1)} %all-to-all-done.1), kind=kOutput, calls=%fused_computation.7 | convolution fusion | flops 101449728 | bytes 1998848 | tf_op jit(solution)/shard_map/erd,erh->edh/dot_general | solution.py:90
  49.3 2.7 %fusion.2 = bf16[1,1,256,3072]{3,2,1,0:T(8,128)(2,1)} fusion(bf16[8,8,3072]{2,1,0:T(8,128)(2,1)} %all-to-all-done, f32[64,256]{1,0:T(8,128)S(1)} %copy-done.4, f32[64,256]{1,0:T(8,128)S(1)} %copy-done.3), kind=kOutput, calls=%fused_computation.8 | convolution fusion | flops 101548032 | bytes 2097152 | tf_op jit(solution)/shard_map/erh,erd->ehd/dot_general | solution.py:80
  52.0 5.6 %all-to-all-done.2 = f32[1,64,3072]{2,0,1:T(1,128)S(1)} async-done(((f32[1,64,3072]{2,0,1:T(1,128)}), f32[1,64,3072]{2,0,1:T(1,128)S(1)}, u32[]{:S(2)}, u32[]{:S(2)}) %all-to-all-start.2) | async-done | bytes 786464 | tf_op jit(solution)/shard_map/all_to_all | solution.py:97
  57.6 3.3 %all-to-all-start.3 = ((f32[1,8,8]{2,0,1:T(1,128)}), f32[1,8,8]{2,0,1:T(1,128)S(1)}, u32[]{:S(2)}, u32[]{:S(2)}) async-start(f32[1,8,8]{2,0,1:T(1,128)} %bitcast.25), calls=%async_computation.3 | async-start | bytes 8192 | tf_op jit(solution)/shard_map/all_to_all | solution.py:98
  60.9 0.1 copy.37
  61.1 1.2 %convolution_convert_fusion.3 = bf16[128,3072]{1,0:T(8,128)(2,1)S(1)} fusion(bf16[16,3072]{1,0:T(8,128)(2,1)S(1)} %reduce_sum.52, s32[16]{0:T(128)} %and_select_fusion.2, pred[16]{0:T(512)(128)(4,1)} %copy-done.11), kind=kOutput, calls=%fused_computation.9 | convolution fusion | flops 12980224 | bytes 884816 | tf_op jit(solution)/shard_map/st,sd->td/dot_general | solution.py:108
  62.2 3.7 %collective-permute-start = (bf16[128,3072]{1,0:T(8,128)(2,1)S(1)}, bf16[128,3072]{1,0:T(8,128)(2,1)S(1)}, u32[]{:S(2)}, u32[]{:S(2)}) collective-permute-start(bf16[128,3072]{1,0:T(8,128)(2,1)S(1)} %convolution_convert_fusion.3), channel_id=1, source_target_pairs={{0,24},{8,0},{16,8},{24,16},{1,25},{9,1},{17,9},{25,17},{2,26},{10... | collective-permute-start | bytes 2359304 | tf_op jit(solution)/shard_map/ppermute | solution.py:16
  65.9 2.5 %fusion = bf16[1,1,3072,256]{3,2,1,0:T(8,128)(2,1)} fusion(bf16[64,256]{1,0:T(8,128)(2,1)} %copy-done.6, bf16[8,1,8,3072]{3,2,1,0:T(8,128)(2,1)S(1)} %all-to-all-done.1), kind=kOutput, calls=%fused_computation.6 | convolution fusion | flops 101449728 | bytes 1998848 | tf_op jit(solution)/shard_map/erd,erh->edh/dot_general | solution.py:87
  68.4 0.5 broadcast.371
  68.9 0.7 reduce.29
  69.7 0.7 fusion.46
  70.4 4.4 %fusion.42 = (f32[768]{0:T(1024)S(1)}, s32[768,1]{0,1:T(1,128)S(1)}) fusion(f32[]{:T(128)} %bitcast.35, f32[]{:T(128)} %bitcast.36, f32[]{:T(128)} %bitcast.37, f32[]{:T(128)} %bitcast.38, f32[]{:T(128)} %bitcast.39, f32[]{:T(128)} %bitcast.41, f32[]{:T(128)} %bitcast.40, s32[768,1]{0,1:T(1,128)S(1)} %mul.82, pred[768,1]{0,1:T(4,128)(4,1)S(1)} %lt.81, ...), kind=kLoop, calls=%fused_computation.92 | loop fusion | flops 14592 | bytes 13084 | tf_op jit(solution)/shard_map/gather | solution.py:112
  74.8 0.1 compare_reduce_fusion.9
  74.9 5.6 %select_select_fusion = f32[768]{0:T(1024)S(1)} fusion(pred[768]{0:T(1024)(128)(4,1)S(1)} %get-tuple-element.29, pred[768]{0:T(1024)(128)(4,1)S(1)} %get-tuple-element.28, pred[768]{0:T(1024)(128)(4,1)S(1)} %get-tuple-element.27, pred[768]{0:T(1024)(128)(4,1)S(1)} %get-tuple-element.26, pred[768]{0:T(1024)(128)(4,1)S(1)} %get-tuple-element.25, ...), kind=kLoop, calls=%fused_computation.88 | loop fusion | flops 7680 | bytes 13860 | tf_op jit(solution)/shard_map/gather | solution.py:112
  80.6 0.1 gather.21
  80.7 0.9 %div.29 = f32[1,128,6]{2,1,0:T(8,128)S(1)} divide(f32[1,128,6]{2,1,0:T(8,128)S(1)} %gather.21, f32[1,128,6]{2,1,0:T(8,128)} %copy-done.5) | non-fusion elementwise | flops 768 | bytes 9216 | tf_op jit(solution)/shard_map/div | solution.py:112
  81.6 0.7 copy.36
  82.2 1.0 %collective-permute-done = bf16[128,3072]{1,0:T(8,128)(2,1)S(1)} collective-permute-done((bf16[128,3072]{1,0:T(8,128)(2,1)S(1)}, bf16[128,3072]{1,0:T(8,128)(2,1)S(1)}, u32[]{:S(2)}, u32[]{:S(2)}) %collective-permute-start) | collective-permute-done | bytes 786464 | tf_op jit(solution)/shard_map/ppermute | solution.py:16
  83.3 0.9 %copy.48 = bf16[1,128,3072]{2,1,0:T(8,128)(2,1)} copy(bf16[1,128,3072]{2,1,0:T(8,128)(2,1)S(1)} %bitcast.151) | data formatting | bytes 1572864
  (41 shorter events, 0.4 us)
Async XLA Ops:
  0.6 28.6 %copy-start = (bf16[1,1,3072,256]{3,2,1,0:T(8,128)(2,1)S(1)}, bf16[1,1,3072,256]{3,2,1,0:T(8,128)(2,1)}, u32[]{:S(2)}) copy-start(bf16[1,1,3072,256]{3,2,1,0:T(8,128)(2,1)} %param.11) | copy-start | bytes 4718596
  3.1 0.5 copy-start.11
  3.2 0.5 copy-start.13
  3.7 12.3 %copy-start.9 = (s32[1,128,6]{1,0,2:T(1,128)S(1)}, s32[1,128,6]{1,0,2:T(1,128)}, u32[]{:S(2)}) copy-start(s32[1,128,6]{1,0,2:T(1,128)} %param.9) | copy-start | bytes 9220
  3.7 12.6 %copy-start.10 = (f32[1,128,6]{1,0,2:T(1,128)S(1)}, f32[1,128,6]{1,0,2:T(1,128)}, u32[]{:S(2)}) copy-start(f32[1,128,6]{1,0,2:T(1,128)} %param.10) | copy-start | bytes 9220
  5.7 11.6 %copy-start.2 = (bf16[1,128,3072]{2,1,0:T(8,128)(2,1)S(1)}, bf16[1,128,3072]{2,1,0:T(8,128)(2,1)}, u32[]{:S(2)}) copy-start(bf16[1,128,3072]{2,1,0:T(8,128)(2,1)} %param.8) | copy-start | bytes 2359300
  10.8 12.6 %all-to-all-start.1 = ((bf16[8,1,8,3072]{3,2,1,0:T(8,128)(2,1)}), bf16[8,1,8,3072]{3,2,1,0:T(8,128)(2,1)S(1)}, u32[]{:S(2)}, u32[]{:S(2)}) async-start(bf16[8,1,8,3072]{3,2,1,0:T(8,128)(2,1)} %fusion.23), calls=%async_computation.1 | async-start | bytes 786432 | tf_op jit(solution)/shard_map/all_to_all | solution.py:9
  16.5 1.5 %copy-start.5 = (f32[1,128,6]{2,1,0:T(8,128)}, f32[1,128,6]{2,1,0:T(8,128)S(1)}, u32[]{:S(2)}) copy-start(f32[1,128,6]{2,1,0:T(8,128)S(1)} %copy.30) | copy-start | bytes 9220
  18.7 11.5 %copy-start.1 = (bf16[1,1,3072,256]{3,2,1,0:T(8,128)(2,1)S(1)}, bf16[1,1,3072,256]{3,2,1,0:T(8,128)(2,1)}, u32[]{:S(2)}) copy-start(bf16[1,1,3072,256]{3,2,1,0:T(8,128)(2,1)} %param.12) | copy-start | bytes 4718596
  25.1 11.5 %all-to-all-start = ((bf16[8,8,3072]{2,1,0:T(8,128)(2,1)}), bf16[8,8,3072]{2,1,0:T(8,128)(2,1)}, u32[]{:S(2)}, u32[]{:S(2)}) async-start(bf16[8,8,3072]{2,1,0:T(8,128)(2,1)} %bitcast.148), calls=%async_computation | async-start | bytes 786432 | tf_op jit(solution)/shard_map/all_to_all | solution.py:64
  39.3 0.6 copy-start.6
  39.3 0.6 copy-start.7
  40.5 5.7 %copy-start.14 = (s32[16]{0:T(128)S(1)}, s32[16]{0:T(128)}, u32[]{:S(2)}) copy-start(s32[16]{0:T(128)} %copy-done.13) | copy-start | bytes 196
  40.6 6.3 %copy-start.12 = (f32[64]{0:T(128)S(1)}, f32[64]{0:T(128)}, u32[]{:S(2)}) copy-start(f32[64]{0:T(128)} %get-tuple-element.32) | copy-start | bytes 772
  40.6 7.0 %copy-start.8 = (bf16[64,256]{1,0:T(8,128)(2,1)S(1)}, bf16[64,256]{1,0:T(8,128)(2,1)}, u32[]{:S(2)}) copy-start(bf16[64,256]{1,0:T(8,128)(2,1)} %copy-done.7) | copy-start | bytes 98308
  42.3 7.0 %copy-start.3 = (f32[64,256]{1,0:T(8,128)S(1)}, f32[64,256]{1,0:T(8,128)}, u32[]{:S(2)}) copy-start(f32[64,256]{1,0:T(8,128)} %fusion.6) | copy-start | bytes 196612
  42.3 7.0 %copy-start.4 = (f32[64,256]{1,0:T(8,128)S(1)}, f32[64,256]{1,0:T(8,128)}, u32[]{:S(2)}) copy-start(f32[64,256]{1,0:T(8,128)} %fusion.9) | copy-start | bytes 196612
  42.3 15.3 %all-to-all-start.2 = ((f32[1,64,3072]{2,0,1:T(1,128)}), f32[1,64,3072]{2,0,1:T(1,128)S(1)}, u32[]{:S(2)}, u32[]{:S(2)}) async-start(f32[1,64,3072]{2,0,1:T(1,128)} %copy.31), calls=%async_computation.2 | async-start | bytes 1572864 | tf_op jit(solution)/shard_map/all_to_all | solution.py:97
  57.6 10.8 %all-to-all-start.3 = ((f32[1,8,8]{2,0,1:T(1,128)}), f32[1,8,8]{2,0,1:T(1,128)S(1)}, u32[]{:S(2)}, u32[]{:S(2)}) async-start(f32[1,8,8]{2,0,1:T(1,128)} %bitcast.25), calls=%async_computation.3 | async-start | bytes 8192 | tf_op jit(solution)/shard_map/all_to_all | solution.py:98
  62.2 21.0 %collective-permute-start = (bf16[128,3072]{1,0:T(8,128)(2,1)S(1)}, bf16[128,3072]{1,0:T(8,128)(2,1)S(1)}, u32[]{:S(2)}, u32[]{:S(2)}) collective-permute-start(bf16[128,3072]{1,0:T(8,128)(2,1)S(1)} %convolution_convert_fusion.3), channel_id=1, source_target_pairs={{0,24},{8,0},{16,8},{24,16},{1,25},{9,1},{17,9},{25,17},{2,26},{10... | collective-permute-start | bytes 2359304 | tf_op jit(solution)/shard_map/ppermute | solution.py:16
